TPU v7x, 512 devices: a whole 4x4x16 slice. The times are simulated.
512 devices in a mesh: src: 32 (over y, x, core), tgt: 16 (over z).
Axes of the slice: x: 4, y: 4, z: 16, core: 2. Of those that a mesh axis runs over, the one named last changes fastest.
Arguments:
- src_cells: float32 [50, 131072], P(None, ('src', 'tgt')), may hold values from -0.8 to 0.8
- tgt_cells: float32 [50, 8192], P(None, 'tgt'), may hold values from -0.8 to 0.8
- src_mass: float32 [131072], P('src'), may hold values from 0.5 to 2
- tgt_mass: float32 [8192], P('tgt'), may hold values from 0.5 to 2
Outputs:
- src_potential: float32 [131072], P('src')
- tgt_potential: float32 [8192], P('tgt')
All inputs are finite; a program needn't handle non-finite values.
Results may differ from a plain program's by a relative error of at most 0.00015.
Values sent between devices are 32-bit elements; how exact they have to be, the bound alone decides.
No kernel may reach another device: no remote copies, remote signals or barrier semaphores. Data moves between devices by JAX's collectives and lax.ppermute only.
A program may use at most 64 MiB of HBM per device.

v0:
```python
import jax
import jax.numpy as jnp
from jax import lax
from jax.sharding import PartitionSpec as P

ITERS = 2
epsilon_reg = 2.0


def gibbs_tile(src_block, tgt_block):
    src_norm = jnp.sum(src_block * src_block, axis=0)
    tgt_norm = jnp.sum(tgt_block * tgt_block, axis=0)
    cross = jnp.dot(
        src_block.T, tgt_block, precision=lax.Precision.HIGHEST, preferred_element_type=jnp.float32
    )
    cost = src_norm[:, None] + tgt_norm[None, :] - 2.0 * cross
    return jnp.exp(-cost / epsilon_reg)


def local(src_cells, tgt_cells, src_mass, tgt_mass):
    src_block = lax.all_gather(src_cells, "tgt", axis=1, tiled=True)
    stored_tile = gibbs_tile(src_block, tgt_cells)

    def get_tile():
        return stored_tile

    col_scale = jnp.ones((tgt_cells.shape[1],), jnp.float32)
    row_scale = jnp.ones((src_block.shape[1],), jnp.float32)
    for sweep in range(ITERS):
        row_part = jnp.dot(get_tile(), col_scale, precision=lax.Precision.HIGHEST)
        row_total = lax.psum(row_part, "tgt")
        row_scale = src_mass / row_total
        col_part = jnp.dot(row_scale, get_tile(), precision=lax.Precision.HIGHEST)
        col_total = lax.psum(col_part, "src")
        col_scale = tgt_mass / col_total
    return (epsilon_reg * jnp.log(row_scale), epsilon_reg * jnp.log(col_scale))


def solution(mesh):
    placed = (P(None, ("src", "tgt")), P(None, "tgt"), P("src"), P("tgt"))
    return jax.shard_map(
        local, mesh=mesh, in_specs=placed, out_specs=(P("src"), P("tgt")), check_vma=False
    )
```

profile of v0, /device:TPU:1, one launch (start us, length us, event | category | flops | bytes accessed | tf_op | source)
XLA Modules:
  0.0 317.8 jit_solution(1861517863350990255)
XLA Ops:
  0.6 0.9 multiply_reduce_fusion.1
  1.6 34.9 %all_gather.3 = f32[50,4096]{1,0:T(8,128)S(1)} all-gather(f32[50,256]{1,0:T(8,128)} %param.4), channel_id=1, replica_groups=mesh['src'=32,'tgt'=16] {'tgt'}, dimensions={1}, use_global_device_ids=true | all-gather | bytes 870400 | tf_op jit(solution)/shard_map/all_gather | solution.py:21
  36.4 0.1 multiply_reduce_fusion
  36.5 9.2 %multiply_exponential_fusion = f32[4096,512]{1,0:T(8,128)S(1)} fusion(f32[50,4096]{1,0:T(8,128)S(1)} %all_gather.3, f32[50,512]{1,0:T(8,128)} %param.5, f32[512]{0:T(512)S(1)} %multiply_reduce_fusion.1, f32[4096]{0:T(1024)S(1)} %multiply_reduce_fusion), kind=kOutput, calls=%fused_computation | convolution fusion | flops 1268776960 | bytes 9328640 | tf_op jit(solution)/shard_map/dot_general | solution.py:13
  45.7 0.0 copy-start
  45.7 3.2 %copy-done = f32[4096,512]{1,0:T(8,128)} copy-done((f32[4096,512]{1,0:T(8,128)}, f32[4096,512]{1,0:T(8,128)S(1)}, u32[]{:S(2)}) %copy-start) | copy-done | bytes 8388632
  48.9 0.0 copy-start.1
  48.9 0.0 copy-start.2
  48.9 7.3 %fusion = f32[1,4096]{1,0:T(1,128)S(1)} fusion(f32[4096,512]{1,0:T(8,128)S(1)} %multiply_exponential_fusion), kind=kOutput, calls=%fused_computation.5 | convolution fusion | flops 25165824 | bytes 8404992 | tf_op jit(solution)/shard_map/dot_general | solution.py:30
  56.2 38.9 %psum.28 = f32[4096]{0:T(1024)S(1)} all-reduce(f32[4096]{0:T(1024)S(1)} %bitcast.18), channel_id=1, replica_groups=mesh['src'=32,'tgt'=16] {'tgt'}, use_global_device_ids=true, to_apply=%region_2.0 | all-reduce | flops 4096 | bytes 32768 | tf_op jit(solution)/shard_map/psum | solution.py:31
  95.1 0.0 copy-done.1
  95.1 6.4 %fusion.3 = f32[1,512]{1,0:T(1,128)S(1)} fusion(f32[4096,1]{0,1:T(1,128)S(1)} %bitcast.16, f32[4096,512]{1,0:T(8,128)} %copy-done), kind=kOutput, calls=%fused_computation.8 | convolution fusion | flops 25165824 | bytes 8407040 | tf_op jit(solution)/shard_map/dot_general | solution.py:33
  101.5 83.6 %psum.29 = f32[512]{0:T(512)S(1)} all-reduce(f32[512]{0:T(512)S(1)} %bitcast.22), channel_id=1, replica_groups=mesh['src'=32,'tgt'=16] {'src'}, use_global_device_ids=true, to_apply=%region_3.0 | all-reduce | flops 512 | bytes 4096 | tf_op jit(solution)/shard_map/psum | solution.py:34
  185.1 0.0 copy-done.2
  185.1 9.4 %fusion.4 = f32[1,4096]{1,0:T(1,128)S(1)} fusion(f32[4096,512]{1,0:T(8,128)} %copy-done, f32[512,1]{0,1:T(1,128)S(1)} %bitcast.20), kind=kOutput, calls=%fused_computation.9 | convolution fusion | flops 25165824 | bytes 8407040 | tf_op jit(solution)/shard_map/dot_general | solution.py:30
  194.6 39.5 %psum.30 = f32[4096]{0:T(1024)S(1)} all-reduce(f32[4096]{0:T(1024)S(1)} %bitcast.17), channel_id=1, replica_groups=mesh['src'=32,'tgt'=16] {'tgt'}, use_global_device_ids=true, to_apply=%region_4.0 | all-reduce | flops 4096 | bytes 32768 | tf_op jit(solution)/shard_map/psum | solution.py:31
  234.1 0.6 log_multiply_fusion
  234.7 6.4 %fusion.5 = f32[1,512]{1,0:T(1,128)S(1)} fusion(f32[4096,1]{0,1:T(1,128)S(1)} %bitcast.19, f32[4096,512]{1,0:T(8,128)} %copy-done), kind=kOutput, calls=%fused_computation.10 | convolution fusion | flops 25165824 | bytes 8407040 | tf_op jit(solution)/shard_map/dot_general | solution.py:33
  241.1 76.1 %psum.31 = f32[512]{0:T(512)S(1)} all-reduce(f32[512]{0:T(512)S(1)} %bitcast.21), channel_id=1, replica_groups=mesh['src'=32,'tgt'=16] {'src'}, use_global_device_ids=true, to_apply=%region_5.0 | all-reduce | flops 512 | bytes 4096 | tf_op jit(solution)/shard_map/psum | solution.py:34
  317.2 0.6 log_multiply_fusion.1
  (2 shorter events, 0.0 us)
Async XLA Ops:
  45.7 3.2 %copy-start = (f32[4096,512]{1,0:T(8,128)}, f32[4096,512]{1,0:T(8,128)S(1)}, u32[]{:S(2)}) copy-start(f32[4096,512]{1,0:T(8,128)S(1)} %multiply_exponential_fusion) | copy-start | bytes 25165828
  48.9 46.2 %copy-start.1 = (f32[4096]{0:T(1024)S(1)}, f32[4096]{0:T(1024)}, u32[]{:S(2)}) copy-start(f32[4096]{0:T(1024)} %param.6) | copy-start | bytes 49156
  48.9 136.2 %copy-start.2 = (f32[512]{0:T(512)S(1)}, f32[512]{0:T(512)}, u32[]{:S(2)}) copy-start(f32[512]{0:T(512)} %param.7) | copy-start | bytes 6148
where the time goes:
time: 318 us
  blocking collectives  273 us (86%)
  matrix products  38.6 us (12%)
  local copies, waits for them, and re-layouts  3.22 us (1%)
    psum x2, blocking collectives, local(): col_total = lax.psum(col_part, 'src')  160 us
    psum x2, blocking collectives, local(): row_total = lax.psum(row_part, 'tgt')  78.5 us
    all_gather x1, blocking collectives, local(): src_block = lax.all_gather(src_cells, 'tgt', axis=1, tiled=True)  34.9 us
    dot_general x2, matrix products, local(): row_part = jnp.dot(get_tile(), col_scale, precision=lax.Precision.HIGHEST)  16.7 us
    dot_general x2, matrix products, local(): col_part = jnp.dot(row_scale, get_tile(), precision=lax.Precision.HIGHEST)  12.7 us
    dot_general x1, matrix products, gibbs_tile(): jnp.dot(src_block.T, tgt_block, precision=lax.Precision.HIGHEST, preferre...  9.15 us

commit v1 on v0

--- a/solution.py
+++ b/solution.py
@@ -31,7 +31,11 @@
         row_total = lax.psum(row_part, "tgt")
         row_scale = src_mass / row_total
         col_part = jnp.dot(row_scale, get_tile(), precision=lax.Precision.HIGHEST)
-        col_total = lax.psum(col_part, "src")
+        col_total = col_part
+        for hop in (1, 2, 4, 8, 16):
+            col_total = col_total + lax.ppermute(
+                col_total, "src", [(dev, dev ^ hop) for dev in range(32)]
+            )
         col_scale = tgt_mass / col_total
     return (epsilon_reg * jnp.log(row_scale), epsilon_reg * jnp.log(col_scale))
 

time: 318 us -> 246 us (0.77)
  blocking collectives: 273 us -> 113 us
  starting transfers between devices: 0 us -> 75.6 us
  waiting for transfers between devices: 0 us -> 10.6 us
    psum x2 -> x0, blocking collectives: 160 us -> none  [local(): col_total = lax.psum(col_part, 'src')]
    ppermute x0 -> x10, starting transfers between devices: none -> 75.6 us  [local(): lax.ppermute(col_total, 'src', [(dev, dev ^ hop) for dev in range(32)])]
    ppermute x0 -> x10, waiting for transfers between devices: none -> 10.6 us  [local(): lax.ppermute(col_total, 'src', [(dev, dev ^ hop) for dev in range(32)])]
  transfers between devices with their start and end apart: 0 -> 10, of which waited for: 0 -> 10; matrix products, arithmetic and copies ran while one was open for 0% -> 0% of each run, Pallas kernels for 0% -> 0%
where the time goes in v1:
time: 246 us; the launch traced here: 243 us
  blocking collectives  113 us (46%)
  starting transfers between devices  75.6 us (31%)
  matrix products  37.2 us (15%)
  waiting for transfers between devices  10.6 us (4%)
  local copies, waits for them, and re-layouts  3.22 us (1%)
    psum x2, blocking collectives, local(): row_total = lax.psum(row_part, 'tgt')  78.1 us
    ppermute x10, starting transfers between devices, local(): lax.ppermute(col_total, 'src', [(dev, dev ^ hop) for dev in range(32)])  75.6 us
    all_gather x1, blocking collectives, local(): src_block = lax.all_gather(src_cells, 'tgt', axis=1, tiled=True)  34.9 us
    dot_general x2, matrix products, local(): row_part = jnp.dot(get_tile(), col_scale, precision=lax.Precision.HIGHEST)  14.5 us
    dot_general x2, matrix products, local(): col_part = jnp.dot(row_scale, get_tile(), precision=lax.Precision.HIGHEST)  13.6 us
    ppermute x10, waiting for transfers between devices, local(): lax.ppermute(col_total, 'src', [(dev, dev ^ hop) for dev in range(32)])  10.6 us
    dot_general x1, matrix products, gibbs_tile(): jnp.dot(src_block.T, tgt_block, precision=lax.Precision.HIGHEST, preferre...  9.15 us
  transfers between devices with their start and end apart: 10, of which 10 were waited for; matrix products, arithmetic and copies ran while one was open for 0% of the time, Pallas kernels for 0%

profile of v1, /device:TPU:1, one launch (start us, length us, event | category | flops | bytes accessed | tf_op | source)
XLA Modules:
  0.0 242.6 jit_solution(16443424744875444006)
XLA Ops:
  1.6 34.9 %all_gather.3 = f32[50,4096]{1,0:T(8,128)S(1)} all-gather(f32[50,256]{1,0:T(8,128)} %param.4), channel_id=1, replica_groups=mesh['src'=32,'tgt'=16] {'tgt'}, dimensions={1}, use_global_device_ids=true | all-gather | bytes 870400 | tf_op jit(solution)/shard_map/all_gather | solution.py:21
  36.5 9.2 %multiply_exponential_fusion = f32[4096,512]{1,0:T(8,128)S(1)} fusion(f32[50,4096]{1,0:T(8,128)S(1)} %all_gather.3, f32[50,512]{1,0:T(8,128)} %param.5, f32[512]{0:T(512)S(1)} %multiply_reduce_fusion.1, f32[4096]{0:T(1024)S(1)} %multiply_reduce_fusion), kind=kOutput, calls=%fused_computation | convolution fusion | flops 1268776960 | bytes 9328640 | tf_op jit(solution)/shard_map/dot_general | solution.py:13
  45.7 3.2 %copy-done = f32[4096,512]{1,0:T(8,128)} copy-done((f32[4096,512]{1,0:T(8,128)}, f32[4096,512]{1,0:T(8,128)S(1)}, u32[]{:S(2)}) %copy-start) | copy-done | bytes 8388632
  48.9 7.3 %fusion = f32[1,4096]{1,0:T(1,128)S(1)} fusion(f32[4096,512]{1,0:T(8,128)S(1)} %multiply_exponential_fusion), kind=kOutput, calls=%fused_computation.7 | convolution fusion | flops 25165824 | bytes 8404992 | tf_op jit(solution)/shard_map/dot_general | solution.py:30
  56.2 38.9 %psum.14 = f32[4096]{0:T(1024)S(1)} all-reduce(f32[4096]{0:T(1024)S(1)} %bitcast.18), channel_id=1, replica_groups=mesh['src'=32,'tgt'=16] {'tgt'}, use_global_device_ids=true, to_apply=%region_2.0 | all-reduce | flops 4096 | bytes 32768 | tf_op jit(solution)/shard_map/psum | solution.py:31
  95.1 7.2 %fusion.3 = f32[1,512]{1,0:T(1,128)S(1)} fusion(f32[4096,1]{0,1:T(1,128)S(1)} %bitcast.16, f32[4096,512]{1,0:T(8,128)} %copy-done), kind=kOutput, calls=%fused_computation.10 | convolution fusion | flops 25165824 | bytes 8407040 | tf_op jit(solution)/shard_map/dot_general | solution.py:33
  102.3 23.2 %collective-permute-start = (f32[512]{0:T(512)S(1)}, f32[512]{0:T(512)S(1)}, u32[]{:S(2)}, u32[]{:S(2)}) collective-permute-start(f32[512]{0:T(512)S(1)} %bitcast.22), channel_id=1, source_target_pairs={{0,16},{16,0},{32,48},{48,32},{64,80},{80,64},{96,112},{112,96},{1... | collective-permute-start | bytes 6152 | tf_op jit(solution)/shard_map/ppermute | solution.py:36
  126.4 3.1 %collective-permute-start.1 = (f32[512]{0:T(512)S(1)}, f32[512]{0:T(512)S(1)}, u32[]{:S(2)}, u32[]{:S(2)}) collective-permute-start(f32[512]{0:T(512)S(1)} %add.50), channel_id=1, source_target_pairs={{0,32},{16,48},{32,0},{48,16},{64,96},{80,112},{96,64},{112,80},{1... | collective-permute-start | bytes 6152 | tf_op jit(solution)/shard_map/ppermute | solution.py:36
  129.5 1.2 collective-permute-done.1
  130.7 4.6 %collective-permute-start.2 = (f32[512]{0:T(512)S(1)}, f32[512]{0:T(512)S(1)}, u32[]{:S(2)}, u32[]{:S(2)}) collective-permute-start(f32[512]{0:T(512)S(1)} %add.51), channel_id=1, source_target_pairs={{0,64},{16,80},{32,96},{48,112},{64,0},{80,16},{96,32},{112,48},{1... | collective-permute-start | bytes 6152 | tf_op jit(solution)/shard_map/ppermute | solution.py:36
  135.4 1.2 collective-permute-done.2
  136.5 3.2 %collective-permute-start.3 = (f32[512]{0:T(512)S(1)}, f32[512]{0:T(512)S(1)}, u32[]{:S(2)}, u32[]{:S(2)}) collective-permute-start(f32[512]{0:T(512)S(1)} %add.52), channel_id=1, source_target_pairs={{0,128},{16,144},{32,160},{48,176},{64,192},{80,208},{96,224},{112... | collective-permute-start | bytes 6152 | tf_op jit(solution)/shard_map/ppermute | solution.py:36
  139.7 1.1 collective-permute-done.3
  140.9 4.8 %collective-permute-start.4 = (f32[512]{0:T(512)S(1)}, f32[512]{0:T(512)S(1)}, u32[]{:S(2)}, u32[]{:S(2)}) collective-permute-start(f32[512]{0:T(512)S(1)} %add.53), channel_id=1, source_target_pairs={{0,256},{16,272},{32,288},{48,304},{64,320},{80,336},{96,352},{112... | collective-permute-start | bytes 6152 | tf_op jit(solution)/shard_map/ppermute | solution.py:36
  146.7 7.2 %fusion.4 = f32[1,4096]{1,0:T(1,128)S(1)} fusion(f32[4096,512]{1,0:T(8,128)S(1)} %copy-done.1, f32[512,1]{0,1:T(1,128)S(1)} %bitcast.24), kind=kOutput, calls=%fused_computation.11 | convolution fusion | flops 25165824 | bytes 8407040 | tf_op jit(solution)/shard_map/dot_general | solution.py:30
  153.9 39.2 %psum.15 = f32[4096]{0:T(1024)S(1)} all-reduce(f32[4096]{0:T(1024)S(1)} %bitcast.17), channel_id=1, replica_groups=mesh['src'=32,'tgt'=16] {'tgt'}, use_global_device_ids=true, to_apply=%region_3.0 | all-reduce | flops 4096 | bytes 32768 | tf_op jit(solution)/shard_map/psum | solution.py:31
  193.7 6.4 %fusion.5 = f32[1,512]{1,0:T(1,128)S(1)} fusion(f32[4096,1]{0,1:T(1,128)S(1)} %bitcast.19, f32[4096,512]{1,0:T(8,128)} %copy-done), kind=kOutput, calls=%fused_computation.12 | convolution fusion | flops 25165824 | bytes 8407040 | tf_op jit(solution)/shard_map/dot_general | solution.py:33
  200.1 20.9 %collective-permute-start.5 = (f32[512]{0:T(512)S(1)}, f32[512]{0:T(512)S(1)}, u32[]{:S(2)}, u32[]{:S(2)}) collective-permute-start(f32[512]{0:T(512)S(1)} %bitcast.20), channel_id=1, source_target_pairs={{0,16},{16,0},{32,48},{48,32},{64,80},{80,64},{96,112},{112,96},{1... | collective-permute-start | bytes 6152 | tf_op jit(solution)/shard_map/ppermute | solution.py:36
  221.7 3.1 %collective-permute-start.6 = (f32[512]{0:T(512)S(1)}, f32[512]{0:T(512)S(1)}, u32[]{:S(2)}, u32[]{:S(2)}) collective-permute-start(f32[512]{0:T(512)S(1)} %add.55), channel_id=1, source_target_pairs={{0,32},{16,48},{32,0},{48,16},{64,96},{80,112},{96,64},{112,80},{1... | collective-permute-start | bytes 6152 | tf_op jit(solution)/shard_map/ppermute | solution.py:36
  224.8 1.2 collective-permute-done.6
  226.0 4.6 %collective-permute-start.7 = (f32[512]{0:T(512)S(1)}, f32[512]{0:T(512)S(1)}, u32[]{:S(2)}, u32[]{:S(2)}) collective-permute-start(f32[512]{0:T(512)S(1)} %add.56), channel_id=1, source_target_pairs={{0,64},{16,80},{32,96},{48,112},{64,0},{80,16},{96,32},{112,48},{1... | collective-permute-start | bytes 6152 | tf_op jit(solution)/shard_map/ppermute | solution.py:36
  230.7 1.2 collective-permute-done.7
  231.9 3.2 %collective-permute-start.8 = (f32[512]{0:T(512)S(1)}, f32[512]{0:T(512)S(1)}, u32[]{:S(2)}, u32[]{:S(2)}) collective-permute-start(f32[512]{0:T(512)S(1)} %add.57), channel_id=1, source_target_pairs={{0,128},{16,144},{32,160},{48,176},{64,192},{80,208},{96,224},{112... | collective-permute-start | bytes 6152 | tf_op jit(solution)/shard_map/ppermute | solution.py:36
  236.2 4.8 %collective-permute-start.9 = (f32[512]{0:T(512)S(1)}, f32[512]{0:T(512)S(1)}, u32[]{:S(2)}, u32[]{:S(2)}) collective-permute-start(f32[512]{0:T(512)S(1)} %add.58), channel_id=1, source_target_pairs={{0,256},{16,272},{32,288},{48,304},{64,320},{80,336},{96,352},{112... | collective-permute-start | bytes 6152 | tf_op jit(solution)/shard_map/ppermute | solution.py:36
  (26 shorter events, 7.0 us)
Async XLA Ops:
  45.7 3.2 %copy-start = (f32[4096,512]{1,0:T(8,128)}, f32[4096,512]{1,0:T(8,128)S(1)}, u32[]{:S(2)}) copy-start(f32[4096,512]{1,0:T(8,128)S(1)} %multiply_exponential_fusion) | copy-start | bytes 25165828
  48.9 46.2 %copy-start.2 = (f32[4096]{0:T(1024)S(1)}, f32[4096]{0:T(1024)}, u32[]{:S(2)}) copy-start(f32[4096]{0:T(1024)} %param.6) | copy-start | bytes 49156
  48.9 97.8 %copy-start.3 = (f32[512]{0:T(512)S(1)}, f32[512]{0:T(512)}, u32[]{:S(2)}) copy-start(f32[512]{0:T(512)} %param.7) | copy-start | bytes 6148
  95.1 51.6 %copy-start.1 = (f32[4096,512]{1,0:T(8,128)S(1)}, f32[4096,512]{1,0:T(8,128)}, u32[]{:S(2)}) copy-start(f32[4096,512]{1,0:T(8,128)} %copy-done) | copy-start | bytes 25165828
  102.3 24.0 %collective-permute-start = (f32[512]{0:T(512)S(1)}, f32[512]{0:T(512)S(1)}, u32[]{:S(2)}, u32[]{:S(2)}) collective-permute-start(f32[512]{0:T(512)S(1)} %bitcast.22), channel_id=1, source_target_pairs={{0,16},{16,0},{32,48},{48,32},{64,80},{80,64},{96,112},{112,96},{1... | collective-permute-start | bytes 6152 | tf_op jit(solution)/shard_map/ppermute | solution.py:36
  126.4 4.3 %collective-permute-start.1 = (f32[512]{0:T(512)S(1)}, f32[512]{0:T(512)S(1)}, u32[]{:S(2)}, u32[]{:S(2)}) collective-permute-start(f32[512]{0:T(512)S(1)} %add.50), channel_id=1, source_target_pairs={{0,32},{16,48},{32,0},{48,16},{64,96},{80,112},{96,64},{112,80},{1... | collective-permute-start | bytes 6152 | tf_op jit(solution)/shard_map/ppermute | solution.py:36
  130.7 5.8 %collective-permute-start.2 = (f32[512]{0:T(512)S(1)}, f32[512]{0:T(512)S(1)}, u32[]{:S(2)}, u32[]{:S(2)}) collective-permute-start(f32[512]{0:T(512)S(1)} %add.51), channel_id=1, source_target_pairs={{0,64},{16,80},{32,96},{48,112},{64,0},{80,16},{96,32},{112,48},{1... | collective-permute-start | bytes 6152 | tf_op jit(solution)/shard_map/ppermute | solution.py:36
  136.5 4.3 %collective-permute-start.3 = (f32[512]{0:T(512)S(1)}, f32[512]{0:T(512)S(1)}, u32[]{:S(2)}, u32[]{:S(2)}) collective-permute-start(f32[512]{0:T(512)S(1)} %add.52), channel_id=1, source_target_pairs={{0,128},{16,144},{32,160},{48,176},{64,192},{80,208},{96,224},{112... | collective-permute-start | bytes 6152 | tf_op jit(solution)/shard_map/ppermute | solution.py:36
  140.9 5.8 %collective-permute-start.4 = (f32[512]{0:T(512)S(1)}, f32[512]{0:T(512)S(1)}, u32[]{:S(2)}, u32[]{:S(2)}) collective-permute-start(f32[512]{0:T(512)S(1)} %add.53), channel_id=1, source_target_pairs={{0,256},{16,272},{32,288},{48,304},{64,320},{80,336},{96,352},{112... | collective-permute-start | bytes 6152 | tf_op jit(solution)/shard_map/ppermute | solution.py:36
  200.1 21.7 %collective-permute-start.5 = (f32[512]{0:T(512)S(1)}, f32[512]{0:T(512)S(1)}, u32[]{:S(2)}, u32[]{:S(2)}) collective-permute-start(f32[512]{0:T(512)S(1)} %bitcast.20), channel_id=1, source_target_pairs={{0,16},{16,0},{32,48},{48,32},{64,80},{80,64},{96,112},{112,96},{1... | collective-permute-start | bytes 6152 | tf_op jit(solution)/shard_map/ppermute | solution.py:36
  221.7 4.3 %collective-permute-start.6 = (f32[512]{0:T(512)S(1)}, f32[512]{0:T(512)S(1)}, u32[]{:S(2)}, u32[]{:S(2)}) collective-permute-start(f32[512]{0:T(512)S(1)} %add.55), channel_id=1, source_target_pairs={{0,32},{16,48},{32,0},{48,16},{64,96},{80,112},{96,64},{112,80},{1... | collective-permute-start | bytes 6152 | tf_op jit(solution)/shard_map/ppermute | solution.py:36
  226.0 5.8 %collective-permute-start.7 = (f32[512]{0:T(512)S(1)}, f32[512]{0:T(512)S(1)}, u32[]{:S(2)}, u32[]{:S(2)}) collective-permute-start(f32[512]{0:T(512)S(1)} %add.56), channel_id=1, source_target_pairs={{0,64},{16,80},{32,96},{48,112},{64,0},{80,16},{96,32},{112,48},{1... | collective-permute-start | bytes 6152 | tf_op jit(solution)/shard_map/ppermute | solution.py:36
  231.9 4.3 %collective-permute-start.8 = (f32[512]{0:T(512)S(1)}, f32[512]{0:T(512)S(1)}, u32[]{:S(2)}, u32[]{:S(2)}) collective-permute-start(f32[512]{0:T(512)S(1)} %add.57), channel_id=1, source_target_pairs={{0,128},{16,144},{32,160},{48,176},{64,192},{80,208},{96,224},{112... | collective-permute-start | bytes 6152 | tf_op jit(solution)/shard_map/ppermute | solution.py:36
  236.2 5.8 %collective-permute-start.9 = (f32[512]{0:T(512)S(1)}, f32[512]{0:T(512)S(1)}, u32[]{:S(2)}, u32[]{:S(2)}) collective-permute-start(f32[512]{0:T(512)S(1)} %add.58), channel_id=1, source_target_pairs={{0,256},{16,272},{32,288},{48,304},{64,320},{80,336},{96,352},{112... | collective-permute-start | bytes 6152 | tf_op jit(solution)/shard_map/ppermute | solution.py:36
